TPU v7x, 32 devices: a whole 2x2x4 slice. The times are simulated.
32 devices in a mesh: dom: 8 (over z, y), cluster: 4 (over x, core).
Axes of the slice: x: 2, y: 2, z: 4, core: 2. Of those that a mesh axis runs over, the one named last changes fastest.
Arguments:
- features: bfloat16 [4, 6144, 512], P('cluster', 'dom'), may hold values from -6 to 6
- stale: bfloat16 [4, 256, 512], P('cluster'), may hold values from -6 to 6
- boundary: int32 [4, 8], P('cluster', 'dom'), may hold values from 0 to 23
- skip: int32 [4, 8], P('cluster'), may hold values 0 or 1
- tile_vals: bfloat16 [4, 256, 32, 128], P('cluster', 'dom'), may hold values from -0.4375 to 0.4375
- tile_row: int32 [4, 256], P('cluster', 'dom'), may hold values from 0 to 5
- tile_src: int32 [4, 256], P('cluster', 'dom'), may hold values from 0 to 9
- tile_count: int32 [4, 8], P('cluster', 'dom'), may hold values from 16 to 32, as said below
- weight: bfloat16 [512, 512], replicated, may hold values from -0.25 to 0.25
- cotangent: bfloat16 [4, 6144, 512], P('cluster', 'dom'), may hold values from -6 to 6
Outputs:
- out_features: bfloat16 [4, 6144, 512], P('cluster', 'dom')
- grad_features: bfloat16 [4, 6144, 512], P('cluster', 'dom')
- grad_weight: float32 [512, 512], P('dom')
Inputs may be any that keep to these rules, and one draw needn't show every extreme that they name: `tile_count`: every partition has at least half of its slots live; some partition has all 32 slots live.
All inputs are finite; a program needn't handle non-finite values. No bound on the sum of `skip` on one device may be relied on, other than what follows from the above.
Results may differ from a plain program's by a relative error of at most 0.02.
Values may be sent and summed in bfloat16 or wider, within the bound.
A program may use at most 64 MiB of HBM per device.

v0:
```python
import jax
import jax.numpy as jnp
from jax import lax
from jax.sharding import PartitionSpec as P


def padded(cells, sides, width):
    for axis, dim in sides:
        count = lax.axis_size(axis)
        head = lax.slice_in_dim(cells, 0, width, axis=dim)
        tail = lax.slice_in_dim(cells, cells.shape[dim] - width, cells.shape[dim], axis=dim)
        cells = jnp.concatenate(
            [
                lax.ppermute(tail, axis, [(i, (i + 1) % count) for i in range(count)]),
                cells,
                lax.ppermute(head, axis, [((i + 1) % count, i) for i in range(count)]),
            ],
            axis=dim,
        )
    return cells


def passed_along(x, axis, by):
    count = lax.axis_size(axis)
    return lax.ppermute(x, axis, [(i, (i + by) % count) for i in range(count)])


def silu_parts(value):
    sig = jax.nn.sigmoid(value)
    return (value * sig, sig * (1.0 + value * (1.0 - sig)))


def per_device(
    features, stale, boundary, skip, tile_vals, tile_row, tile_src, tile_count, weight, cotangent
):
    feats = features[0]
    nodes, width = feats.shape
    parts = lax.axis_size("dom")
    blk = stale.shape[1] // parts
    tile_blocks = tile_vals[0]
    slots, _, tile_rows = tile_blocks.shape
    row_blocks = nodes // tile_rows
    start_row = boundary[0, 0] * blk
    own_block = lax.dynamic_slice_in_dim(feats, start_row, blk, 0)
    gathered = lax.all_gather(own_block, "dom", axis=0, tiled=True).reshape(parts, blk, width)
    beside_all = padded(own_block[None], (("cluster", 0),), 1)
    skipped = skip[0] == 1
    fresh = jnp.where(skipped[:, None, None], stale[0].reshape(parts, blk, width), gathered)
    table = jnp.concatenate([fresh, beside_all[0:1], beside_all[2:3]], axis=0)
    active_mask = (jnp.arange(slots, dtype=jnp.int32) < tile_count[0, 0]).astype(jnp.float32)
    sources = tile_src[0]
    targets = tile_row[0]
    selected_block = jnp.take(table, sources, axis=0)
    contribution = (
        jnp.einsum("wnz,wnx->wzx", tile_blocks, selected_block, preferred_element_type=jnp.float32)
        * active_mask[:, None, None]
    )
    row_onehot_mask = (targets[:, None] == jnp.arange(row_blocks, dtype=jnp.int32)[None, :]).astype(
        jnp.float32
    )
    row_onehot_mask = row_onehot_mask * active_mask[:, None]
    aggregate_block_list = jnp.einsum(
        "xn,xij->nij", row_onehot_mask, contribution, precision=lax.Precision.HIGHEST
    )
    agg = (feats.astype(jnp.float32) + aggregate_block_list.reshape(nodes, width)).astype(
        jnp.bfloat16
    )
    zval = jnp.dot(agg, weight, preferred_element_type=jnp.float32)
    act, slope = silu_parts(zval)
    out_features = act.astype(jnp.bfloat16)
    dz = (cotangent[0].astype(jnp.float32) * slope).astype(jnp.bfloat16)
    dagg = lax.dot_general(
        dz, weight, (((1,), (1,)), ((), ())), preferred_element_type=jnp.float32
    ).astype(jnp.bfloat16)
    selected_rows = jnp.take(dagg.reshape(row_blocks, tile_rows, width), targets, axis=0)
    selected_gradient = (
        jnp.einsum("dck,dkn->dcn", tile_blocks, selected_rows, preferred_element_type=jnp.float32)
        * active_mask[:, None, None]
    )
    src_hot = (sources[:, None] == jnp.arange(parts + 2, dtype=jnp.int32)[None, :]).astype(
        jnp.float32
    )
    dsrc = jnp.einsum("ts,tbf->sbf", src_hot, selected_gradient, precision=lax.Precision.HIGHEST)
    keep = 1.0 - skipped.astype(jnp.float32)
    in_group = dsrc[:parts] * keep[:, None, None]
    from_upper = passed_along(dsrc[parts].astype(jnp.bfloat16), "cluster", -1).astype(jnp.float32)
    from_lower = passed_along(dsrc[parts + 1].astype(jnp.bfloat16), "cluster", 1).astype(
        jnp.float32
    )
    share = width // parts
    term_all = lax.dot_general(
        agg, dz, (((0,), (0,)), ((), ())), preferred_element_type=jnp.float32
    ).reshape(parts, share, width)
    stacked = jnp.concatenate([in_group, term_all], axis=1).reshape(parts * (blk + share), width)
    summed = lax.psum_scatter(
        stacked.astype(jnp.bfloat16), "dom", scatter_dimension=0, tiled=True
    ).astype(jnp.float32)
    mine = summed[:blk]
    grad_weight = lax.psum(summed[blk:].astype(jnp.bfloat16), "cluster").astype(jnp.float32)
    bgrad = mine + from_upper + from_lower
    full = dagg.astype(jnp.float32)
    current = lax.dynamic_slice_in_dim(full, start_row, blk, 0)
    full = lax.dynamic_update_slice_in_dim(full, current + bgrad, start_row, 0)
    grad_features = full.astype(jnp.bfloat16)
    return (out_features[None], grad_features[None], grad_weight)


def solution(mesh):
    return jax.shard_map(
        per_device,
        mesh=mesh,
        in_specs=(
            P("cluster", "dom", None),
            P("cluster", None, None),
            P("cluster", "dom"),
            P("cluster", None),
            P("cluster", "dom", None, None),
            P("cluster", "dom"),
            P("cluster", "dom"),
            P("cluster", "dom"),
            P(),
            P("cluster", "dom", None),
        ),
        out_specs=(P("cluster", "dom", None), P("cluster", "dom", None), P("dom", None)),
        check_vma=False,
    )
```

profile of v0, /device:TPU:0, one launch (start us, length us, event | category | flops | bytes accessed | tf_op | source)
XLA Modules:
  0.0 193.5 jit_solution(16718258283287903912)
XLA Ops:
  7.2 0.0 copy-start
  7.2 0.0 reduce-scatter.2.cloned.1.call-start
  8.0 0.8 constant_dynamic-slice_fusion
  8.7 0.5 collective-permute-start
  9.2 1.9 collective-permute-start.1
  11.1 31.9 %all-gather = bf16[1,256,512]{2,1,0:T(8,128)(2,1)S(1)} all-gather(bf16[1,32,512]{2,1,0:T(8,128)(2,1)S(1)} %constant_dynamic-slice_fusion), channel_id=2, replica_groups=mesh['dom'=8,'cluster'=4] {'dom'}, dimensions={1}, use_global_device_ids=true | all-gather | bytes 294912 | tf_op jit(solution)/shard_map/all_gather | solution.py:45
  43.0 0.7 fusion.30
  43.7 0.7 compare_and_fusion.1
  44.3 0.7 fusion.31
  45.0 0.7 compare_and_fusion
  45.7 0.7 compare_bitcast_fusion
  46.3 0.7 convert_subtract_fusion
  47.7 1.1 broadcast_select_fusion
  48.7 0.0 collective-permute-done
  48.7 0.0 collective-permute-done.1
  48.8 0.6 gather_fusion
  49.4 4.6 %fusion.13 = f32[32,512,128]{2,1,0:T(8,128)} fusion(bf16[32,32,512]{2,1,0:T(8,128)(2,1)S(1)} %gather_fusion, pred[32]{0:T(512)(128)(4,1)S(1)} %compare_and_fusion.1, bf16[1,32,32,128]{3,2,1,0:T(8,128)(2,1)S(1)} %copy-done.1), kind=kOutput, calls=%fused_computation.22 | convolution fusion | flops 134742016 | bytes 9699360 | tf_op jit(solution)/shard_map/wnz,wnx->wzx/dot_general | solution.py:55
  54.1 10.3 %copy.20 = f32[32,512,128]{1,0,2:T(8,128)} copy(f32[32,512,128]{2,1,0:T(8,128)} %fusion.13) | data formatting | bytes 16777216 | tf_op jit(solution)/shard_map/wnz,wnx->wzx/dot_general | solution.py:55
  64.4 6.8 %fusion = f32[6,128,512]{2,0,1:T(8,128)S(1)} fusion(f32[32,512,128]{1,0,2:T(8,128)} %copy.20, f32[32]{0:T(128)S(1)} %compare_convert_fusion, s32[32]{0:T(128)S(1)} %bitcast.72), kind=kOutput, calls=%fused_computation.2 | convolution fusion | flops 153092480 | bytes 9961728 | tf_op jit(solution)/shard_map/xn,xij->nij/dot_general | solution.py:62
  71.2 0.0 copy-start.2
  71.2 0.9 copy.16
  72.1 0.2 copy-done.2
  72.3 0.3 fusion.11
  72.6 1.2 copy.17
  73.8 2.0 %fusion.10 = (bf16[768,512]{1,0:T(8,128)(2,1)S(1)}, bf16[1,768,512]{2,1,0:T(8,128)(2,1)}) fusion(bf16[1,768,512]{2,1,0:T(8,128)(2,1)S(1)} %copy-done.7, bf16[768,512]{1,0:T(8,128)(2,1)S(1)} %fusion.11, bf16[512,512]{1,0:T(8,128)(2,1)S(1)} %copy-done), kind=kOutput, calls=%fused_computation.14 | convolution fusion | flops 407371776 | bytes 3670016 | tf_op jit(solution)/shard_map/dot_general | solution.py:68
  75.8 0.6 fusion.35
  76.4 0.5 copy-done.3
  76.9 1.4 convolution_convert_fusion.1
  78.3 2.8 %gather_fusion.1 = bf16[32,128,512]{2,1,0:T(8,128)(2,1)} fusion(bf16[6,128,512]{2,1,0:T(8,128)(2,1)S(1)} %bitcast.66, s32[1024]{0:T(1024)S(1)} %pad_clamp_fusion), kind=kCustom, calls=%fused_computation.1 | custom fusion | bytes 8388736 | tf_op jit(solution)/shard_map/jit(_take)/gather | solution.py:75
  81.0 3.1 %fusion.3 = f32[32,512,32]{1,2,0:T(8,128)S(1)} fusion(bf16[32,128,512]{2,1,0:T(8,128)(2,1)} %gather_fusion.1, pred[32]{0:T(512)(128)(4,1)S(1)} %compare_and_fusion, bf16[1,32,32,128]{3,2,1,0:T(8,128)(2,1)S(1)} %copy-done.1), kind=kOutput, calls=%fused_computation.5 | convolution fusion | flops 136314880 | bytes 6553632 | tf_op jit(solution)/shard_map/dck,dkn->dcn/dot_general | solution.py:77
  84.2 0.0 copy-start.4
  84.2 2.0 %fusion.7 = f32[10,32,512]{2,0,1:T(8,128)S(1)} fusion(f32[32,512,32]{1,2,0:T(8,128)S(1)} %fusion.3, f32[32]{0:T(128)S(1)} %compare_convert_fusion, s32[32]{0:T(128)S(1)} %bitcast.73), kind=kOutput, calls=%fused_computation.9 | convolution fusion | flops 63439168 | bytes 2752768 | tf_op jit(solution)/shard_map/ts,tbf->sbf/dot_general | solution.py:83
  86.2 0.1 fusion.18
  86.3 0.1 copy.18
  86.4 1.0 pad_maximum_fusion
  87.4 0.0 reduce-scatter.2.cloned.1.call-update
  87.4 0.0 all-reduce.2.cloned.1.call-start
  87.4 0.4 copy.27
  87.8 0.1 collective-permute-start.2
  87.9 0.5 collective-permute-start.3
  88.4 63.3 %reduce-scatter.2.cloned.1.call-done = bf16[96,512]{1,0:T(8,128)(2,1)} async-done(((bf16[768,512]{1,0:T(8,128)(2,1)}), bf16[96,512]{1,0:T(8,128)(2,1)}) %reduce-scatter.2.cloned.1.call-update) | async-done | bytes 98320 | tf_op jit(solution)/shard_map/reduce_scatter | solution.py:95
  151.7 1.5 slice.35
  153.2 0.0 all-reduce.2.cloned.1.call-update
  153.2 0.0 collective-permute-done.2
  153.2 0.8 add_dynamic-update-slice_fusion
  154.0 1.0 convert_bitcast_fusion
  155.0 30.2 %all-reduce.2.cloned.1.call-done = bf16[64,512]{1,0:T(8,128)(2,1)} async-done(((bf16[64,512]{1,0:T(8,128)(2,1)}), bf16[64,512]{1,0:T(8,128)(2,1)}) %all-reduce.2.cloned.1.call-update) | async-done | bytes 65552 | tf_op jit(solution)/shard_map/psum | solution.py:99
  185.2 1.5 convert_element_type.90
  (17 shorter events, 0.1 us)
Async XLA Ops:
  7.2 66.6 %copy-start = (bf16[512,512]{1,0:T(8,128)(2,1)S(1)}, bf16[512,512]{1,0:T(8,128)(2,1)}, u32[]{:S(2)}) copy-start(bf16[512,512]{1,0:T(8,128)(2,1)} %param.18) | copy-start | bytes 1572868
  7.2 42.2 %copy-start.1 = (bf16[1,32,32,128]{3,2,1,0:T(8,128)(2,1)S(1)}, bf16[1,32,32,128]{3,2,1,0:T(8,128)(2,1)}, u32[]{:S(2)}) copy-start(bf16[1,32,32,128]{3,2,1,0:T(8,128)(2,1)} %param.14) | copy-start | bytes 786436
  7.2 144.5 %reduce-scatter.2.cloned.1.call-start = ((), (), s32[]{:S(2)}) async-start(), calls=%async_computation.1 | async-start | bytes 884736 | tf_op jit(solution)/shard_map/reduce_scatter | solution.py:95
  8.7 40.0 %collective-permute-start = (bf16[1,32,512]{2,1,0:T(8,128)(2,1)S(1)}, bf16[1,32,512]{2,1,0:T(8,128)(2,1)S(1)}, u32[]{:S(2)}, u32[]{:S(2)}) collective-permute-start(bf16[1,32,512]{2,1,0:T(8,128)(2,1)S(1)} %constant_dynamic-slice_fusion), channel_id=1, source_target_pairs={{0,1},{1,2},{2,3},{3,0},{4,5},{5,6},{6,7},{7,4},{8,9},{9,10},{10,1... | collective-permute-start | bytes 98312 | tf_op jit(solution)/shard_map/ppermute | solution.py:14
  9.2 39.5 %collective-permute-start.1 = (bf16[1,32,512]{2,1,0:T(8,128)(2,1)S(1)}, bf16[1,32,512]{2,1,0:T(8,128)(2,1)S(1)}, u32[]{:S(2)}, u32[]{:S(2)}) collective-permute-start(bf16[1,32,512]{2,1,0:T(8,128)(2,1)S(1)} %constant_dynamic-slice_fusion), channel_id=1, source_target_pairs={{1,0},{2,1},{3,2},{0,3},{5,4},{6,5},{7,6},{4,7},{9,8},{10,9},{11,1... | collective-permute-start | bytes 98312 | tf_op jit(solution)/shard_map/ppermute | solution.py:16
  54.0 10.3 %copy-start.5 = (s32[1,32]{1,0:T(1,128)S(1)}, s32[1,32]{1,0:T(1,128)}, u32[]{:S(2)}) copy-start(s32[1,32]{1,0:T(1,128)} %param.15) | copy-start | bytes 388
  71.2 1.1 copy-start.2
  72.3 1.5 copy-start.7
  75.8 1.1 copy-start.3
  81.0 3.1 %copy-start.6 = (s32[1,32]{1,0:T(1,128)S(1)}, s32[1,32]{1,0:T(1,128)}, u32[]{:S(2)}) copy-start(s32[1,32]{1,0:T(1,128)} %param.16) | copy-start | bytes 388
  84.2 2.2 %copy-start.4 = (bf16[8,64,512]{2,1,0:T(8,128)(2,1)S(1)}, bf16[8,64,512]{2,1,0:T(8,128)(2,1)}, u32[]{:S(2)}) copy-start(bf16[8,64,512]{2,1,0:T(8,128)(2,1)} %convolution_convert_fusion.1) | copy-start | bytes 1572868
  87.4 97.8 %all-reduce.2.cloned.1.call-start = ((), (), s32[]{:S(2)}) async-start(), calls=%async_computation.2 | async-start | bytes 131072 | tf_op jit(solution)/shard_map/psum | solution.py:99
  87.8 65.4 %collective-permute-start.2 = (bf16[32,512]{1,0:T(8,128)(2,1)S(1)}, bf16[32,512]{1,0:T(8,128)(2,1)S(1)}, u32[]{:S(2)}, u32[]{:S(2)}) collective-permute-start(bf16[32,512]{1,0:T(8,128)(2,1)S(1)} %get-tuple-element.5), channel_id=1, source_target_pairs={{0,3},{1,0},{2,1},{3,2},{4,7},{5,4},{6,5},{7,6},{8,11},{9,8},{10,9... | collective-permute-start | bytes 98312 | tf_op jit(solution)/shard_map/ppermute | solution.py:25
  87.9 65.3 %collective-permute-start.3 = (bf16[32,512]{1,0:T(8,128)(2,1)S(1)}, bf16[32,512]{1,0:T(8,128)(2,1)S(1)}, u32[]{:S(2)}, u32[]{:S(2)}) collective-permute-start(bf16[32,512]{1,0:T(8,128)(2,1)S(1)} %get-tuple-element.6), channel_id=1, source_target_pairs={{0,1},{1,2},{2,3},{3,0},{4,5},{5,6},{6,7},{7,4},{8,9},{9,10},{10,1... | collective-permute-start | bytes 98312 | tf_op jit(solution)/shard_map/ppermute | solution.py:25
Sparse Core Ops, SparseCore 0:
  87.5 64.1 reduce-scatter.1
  154.6 30.5 all-reduce.1
where the time goes:
time: 194 us
  waiting for transfers between devices  93.6 us (48%)
  blocking collectives  31.9 us (16%)
  matrix products  20.5 us (11%)
  local copies, waits for them, and re-layouts  19.2 us (10%)
  between operations  15.6 us (8%)
  other arithmetic  9.72 us (5%)
  starting transfers between devices  3.04 us (2%)
    reduce_scatter x1, waiting for transfers between devices, per_device(): lax.psum_scatter(stacked.astype(jnp.bfloat16), 'dom', scatter_dimension=0...  63.3 us
    all_gather x1, blocking collectives, per_device(): lax.all_gather(own_block, 'dom', axis=0, tiled=True)  31.9 us
    psum x1, waiting for transfers between devices, per_device(): lax.psum(summed[blk:].astype(jnp.bfloat16), 'cluster').astype(jnp.float32)  30.2 us
    dot_general x1, local copies, waits for them, and re-layouts, per_device(): jnp.einsum('wnz,wnx->wzx', tile_blocks, selected_block, preferred_element...  10.3 us
    dot_general x1, matrix products, per_device(): jnp.einsum('xn,xij->nij', row_onehot_mask, contribution, precision=lax.Pr...  6.78 us
    dot_general x1, matrix products, per_device(): jnp.einsum('wnz,wnx->wzx', tile_blocks, selected_block, preferred_element...  4.61 us
  transfers between devices with their start and end apart: 6, of which 2 were waited for; matrix products, arithmetic and copies ran while one was open for 4% of the time, Pallas kernels for 0%

commit v1 on v0

v1 whole, which is shorter than its diff:
```python
import functools

import jax
import jax.numpy as jnp
from jax import lax
from jax.experimental import pallas as pl
from jax.experimental.pallas import tpu as pltpu
from jax.sharding import PartitionSpec as P

MESH = pl.DeviceIdType.MESH
F32 = jnp.float32
BF16 = jnp.bfloat16


def dot(a, b, da, db):
    return lax.dot_general(a, b, (((da,), (db,)), ((), ())), preferred_element_type=F32)


def iota(shape, axis):
    return lax.broadcasted_iota(jnp.int32, shape, axis)


def kernel(
    doms,
    clusters,
    bnd,
    skip,
    trow,
    tsrc,
    tcnt,
    feats_h,
    tiles_h,
    stale_h,
    weight_h,
    cot_h,
    out,
    gfeat,
    gw,
    feats,
    tiles,
    stale,
    weight,
    cot,
    own,
    gath,
    table,
    spread,
    picks,
    adj,
    agg,
    dz,
    dagg,
    half_out,
    half_in,
    pair,
    pair_in,
    bg_out,
    bg_in,
    quarter,
    quarter_in,
    load_sem,
    ag_send,
    ag_recv,
    half_send,
    half_recv,
    pair_send,
    pair_recv,
    bg_send,
    bg_recv,
    q_send,
    q_recv,
):
    me = lax.axis_index("dom")
    mine = lax.axis_index("cluster")
    parity = lax.rem(mine, 2)
    nodes, width = feats.shape
    slots, blk, tile_rows = tiles.shape
    row_blocks = nodes // tile_rows
    half = width // 2
    share = width // doms

    def dom_at(k):
        return {"dom": lax.rem(me + k + doms, doms)}

    def cluster_at(k):
        return {"cluster": lax.rem(mine + k + clusters, clusters)}

    loads = []
    for i, (src, dst) in enumerate(
        ((feats_h, feats), (tiles_h, tiles), (stale_h, stale), (weight_h, weight), (cot_h, cot))
    ):
        loads.append(pltpu.make_async_copy(src, dst, load_sem.at[i]))
        loads[-1].start()

    barrier = pltpu.get_barrier_semaphore()
    for k in range(1, doms):
        pl.semaphore_signal(barrier, inc=1, device_id=dom_at(k), device_id_type=MESH)
    for k in range(1, clusters):
        pl.semaphore_signal(barrier, inc=1, device_id=cluster_at(k), device_id_type=MESH)

    loads[0].wait()
    exported = iota((blk, nodes), 1) - iota((blk, nodes), 0) == bnd[0, 0] * blk
    own[...] = dot(jnp.where(exported, 1.0, 0.0).astype(BF16), feats[...], 1, 0).astype(BF16)
    pl.semaphore_wait(barrier, doms - 1 + clusters - 1)

    def remote(src, dst, send, recv, to):
        copy = pltpu.make_async_remote_copy(
            src_ref=src, dst_ref=dst, send_sem=send, recv_sem=recv, device_id=to, device_id_type=MESH
        )
        copy.start()
        return copy

    gathers = []
    for k in range(1, doms):
        gathers.append(
            remote(own, gath.at[k], ag_send.at[k], ag_recv.at[k], dom_at(k))
        )
    for k, by in ((doms, 1), (doms + 1, -1)):
        gathers.append(
            remote(own, gath.at[k], ag_send.at[k], ag_recv.at[k], cluster_at(by))
        )

    loads[1].wait()
    sources = (doms + 2) * blk
    offset = iota((blk, sources), 1) - iota((blk, sources), 0)
    row_block = iota((blk, nodes), 1) // tile_rows
    for t in range(slots):
        at = slice(t * blk, (t + 1) * blk)
        picks[at, :] = jnp.where(offset == tsrc[0, t] * blk, 1.0, 0.0).astype(BF16)
        row = trow[0, t] + nodes * jnp.maximum(t + 1 - tcnt[0, 0], 0)
        block = jnp.concatenate([tiles[t].astype(F32)] * row_blocks, axis=1)
        spread[at, :] = jnp.where(row_block == row, block, 0.0).astype(BF16)
    adj[...] = dot(picks[...], spread[...], 0, 0).astype(BF16)

    loads[2].wait()
    loads[3].wait()
    loads[4].wait()
    one = jnp.ones((blk, width), jnp.int32)

    def block_of(k):
        source = lax.rem(me - k + doms, doms) if k < doms else k
        return source, pl.ds(pl.multiple_of(source * blk, blk), blk)

    for k in range(doms + 2):
        if k > 0:
            gathers[k - 1].wait_recv()
        fresh = own[...] if k == 0 else gath[k]
        source, at = block_of(k)
        if k < doms:
            cached = one == skip[0, source]
            fresh = jnp.where(cached, stale[at, :].astype(F32), fresh.astype(F32)).astype(BF16)
        table[at, :] = fresh

    chunk = 2 * tile_rows
    for r in range(0, nodes, chunk):
        rows = slice(r, r + chunk)
        total = feats[rows, :].astype(F32) + dot(adj[:, rows], table[...], 0, 0)
        total = total.astype(BF16)
        agg[rows, :] = total
        z = dot(total, weight[...], 1, 0)
        sig = 1.0 / (1.0 + jnp.exp(-z))
        act = z * sig
        out[rows, :] = act.astype(BF16)
        dz[rows, :] = (cot[rows, :].astype(F32) * (sig * (1.0 + z * (1.0 - sig)))).astype(BF16)

    def half_at(which):
        return pl.ds(pl.multiple_of(which * half, half), half)

    half_out[...] = dot(agg[...], dz[:, half_at(1 - parity)], 0, 0).astype(BF16)
    partner = {"cluster": mine + 1 - 2 * parity}
    halves = remote(half_out, half_in, half_send.at[0], half_recv.at[0], partner)

    for r in range(0, nodes, chunk):
        rows = slice(r, r + chunk)
        dagg[rows, :] = dot(dz[rows, :], weight[...], 1, 1).astype(BF16)
    dsrc = dot(adj[...], dagg[...], 1, 0)
    for source in range(doms + 2):
        at = slice(source * blk, (source + 1) * blk)
        grad = dsrc[at, :]
        if source < doms:
            grad = jnp.where(one == skip[0, source], 0.0, grad)
        bg_out[at, :] = grad.astype(BF16)
    blocks = []
    for k in range(1, doms + 2):
        to = dom_at(-k) if k < doms else cluster_at(-1 if k == doms else 1)
        blocks.append(
            remote(bg_out.at[block_of(k)[1]], bg_in.at[k], bg_send.at[k], bg_recv.at[k], to)
        )

    wsum = dot(agg[...], dz[:, half_at(parity)], 0, 0)
    halves.wait_recv()
    wsum = wsum + half_in[...].astype(F32)
    pair[...] = wsum.astype(BF16)

    def share_at(k):
        part = lax.rem(me + k + doms, doms)
        return pl.ds(pl.multiple_of(part * share, share), share)

    pairs = []
    for k in range(1, doms):
        pairs.append(
            remote(pair.at[share_at(k)], pair_in.at[k], pair_send.at[k], pair_recv.at[k], dom_at(k))
        )

    bgrad = bg_out[block_of(0)[1], :].astype(F32)
    for k in range(1, doms + 2):
        blocks[k - 1].wait_recv()
        bgrad = bgrad + bg_in[k].astype(F32)
    for b in range(nodes // blk):
        rows = slice(b * blk, (b + 1) * blk)
        here = jnp.where(one * b == bnd[0, 0], bgrad, 0.0)
        gfeat[rows, :] = (dagg[rows, :].astype(F32) + here).astype(BF16)

    rsum = pair[share_at(0), :].astype(F32)
    for k in range(1, doms):
        pairs[k - 1].wait_recv()
        rsum = rsum + pair_in[k].astype(F32)
    quarter[...] = rsum.astype(BF16)
    quarters = []
    for k in range(1, clusters):
        quarters.append(
            remote(quarter, quarter_in.at[k], q_send.at[k], q_recv.at[k], cluster_at(k))
        )
    same = quarter[...].astype(F32)
    other = jnp.zeros_like(same)
    for k in range(1, clusters):
        quarters[k - 1].wait_recv()
        if k % 2 == 0:
            same = same + quarter_in[k].astype(F32)
        else:
            other = other + quarter_in[k].astype(F32)
    gw[:, half_at(parity)] = same
    gw[:, half_at(1 - parity)] = other

    for copy in gathers + [halves] + blocks + pairs + quarters:
        copy.wait_send()


def per_device(
    doms,
    clusters,
    features,
    stale,
    boundary,
    skip,
    tile_vals,
    tile_row,
    tile_src,
    tile_count,
    weight,
    cotangent,
):
    _, nodes, width = features.shape
    _, slots, blk, tile_rows = tile_vals.shape
    half, share = width // 2, width // doms
    smem = pl.BlockSpec(memory_space=pltpu.SMEM)
    vmem = pl.BlockSpec(memory_space=pltpu.VMEM)
    hbm = pl.BlockSpec(memory_space=pl.ANY)
    dma = pltpu.SemaphoreType.DMA
    out, gfeat, gw = pl.pallas_call(
        functools.partial(kernel, doms, clusters),
        out_shape=(
            jax.ShapeDtypeStruct((nodes, width), BF16),
            jax.ShapeDtypeStruct((nodes, width), BF16),
            jax.ShapeDtypeStruct((share, width), F32),
        ),
        in_specs=[smem] * 5 + [hbm] * 5,
        out_specs=(vmem, vmem, vmem),
        scratch_shapes=[
            pltpu.VMEM((nodes, width), BF16),
            pltpu.VMEM((slots, blk, tile_rows), BF16),
            pltpu.VMEM((doms * blk, width), BF16),
            pltpu.VMEM((width, width), BF16),
            pltpu.VMEM((nodes, width), BF16),
            pltpu.VMEM((blk, width), BF16),
            pltpu.VMEM((doms + 2, blk, width), BF16),
            pltpu.VMEM(((doms + 2) * blk, width), BF16),
            pltpu.VMEM((slots * blk, nodes), BF16),
            pltpu.VMEM((slots * blk, (doms + 2) * blk), BF16),
            pltpu.VMEM(((doms + 2) * blk, nodes), BF16),
            pltpu.VMEM((nodes, width), BF16),
            pltpu.VMEM((nodes, width), BF16),
            pltpu.VMEM((nodes, width), BF16),
            pltpu.VMEM((width, half), BF16),
            pltpu.VMEM((width, half), BF16),
            pltpu.VMEM((width, half), BF16),
            pltpu.VMEM((doms, share, half), BF16),
            pltpu.VMEM(((doms + 2) * blk, width), BF16),
            pltpu.VMEM((doms + 2, blk, width), BF16),
            pltpu.VMEM((share, half), BF16),
            pltpu.VMEM((clusters, share, half), BF16),
            dma((5,)),
            dma((doms + 2,)),
            dma((doms + 2,)),
            dma((1,)),
            dma((1,)),
            dma((doms,)),
            dma((doms,)),
            dma((doms + 2,)),
            dma((doms + 2,)),
            dma((clusters,)),
            dma((clusters,)),
        ],
        compiler_params=pltpu.CompilerParams(
            collective_id=0, has_side_effects=True, vmem_limit_bytes=40 * 2**20
        ),
    )(
        boundary,
        skip,
        tile_row,
        tile_src,
        tile_count,
        features[0],
        tile_vals[0],
        stale[0],
        weight,
        cotangent[0],
    )
    return (out[None], gfeat[None], gw)


def solution(mesh):
    return jax.shard_map(
        functools.partial(per_device, mesh.shape["dom"], mesh.shape["cluster"]),
        mesh=mesh,
        in_specs=(
            P("cluster", "dom", None),
            P("cluster", None, None),
            P("cluster", "dom"),
            P("cluster", None),
            P("cluster", "dom", None, None),
            P("cluster", "dom"),
            P("cluster", "dom"),
            P("cluster", "dom"),
            P(),
            P("cluster", "dom", None),
        ),
        out_specs=(P("cluster", "dom", None), P("cluster", "dom", None), P("dom", None)),
        check_vma=False,
    )
```

time: 194 us -> 42.5 us (0.22)
  waiting for transfers between devices: 93.6 us -> 0 us
  Pallas kernels: 0 us -> 31.9 us
  blocking collectives: 31.9 us -> 0 us
  matrix products: 20.5 us -> 0 us
  between operations: 15.6 us -> 1.96 us
  local copies, waits for them, and re-layouts: 19.2 us -> 8.28 us
  other arithmetic: 9.72 us -> 0 us
  starting transfers between devices: 3.04 us -> 0 us
    reduce_scatter x1 -> x0, waiting for transfers between devices: 63.3 us -> none  [per_device(): lax.psum_scatter(stacked.astype(jnp.bfloat16), 'dom', scatter_dimension=0...]
    pallas_call x0 -> x1, Pallas kernels: none -> 31.9 us  [per_device(): pl.pallas_call(functools.partial(kernel, doms, clusters), out_shape=(jax....]
    all_gather x1 -> x0, blocking collectives: 31.9 us -> none  [per_device(): lax.all_gather(own_block, 'dom', axis=0, tiled=True)]
    psum x1 -> x0, waiting for transfers between devices: 30.2 us -> none  [per_device(): lax.psum(summed[blk:].astype(jnp.bfloat16), 'cluster').astype(jnp.float32)]
    dot_general x7 -> x0, matrix products: 20.5 us -> none  [the longest x1 6.78 us: per_device(): jnp.einsum('xn,xij->nij', row_onehot_mask, contribution, precision=lax.Pr...]
    dot_general x4 -> x0, local copies, waits for them, and re-layouts: 12.8 us -> none  [the longest x1 10.3 us: per_device(): jnp.einsum('wnz,wnx->wzx', tile_blocks, selected_block, preferred_element...]
    unnamed x16 -> x19, local copies, waits for them, and re-layouts: 0.76 us -> 8.28 us
    gather x2 -> x0, local copies, waits for them, and re-layouts: 3.38 us -> none  [the longest x1 2.77 us: per_device(): jnp.take(dagg.reshape(row_blocks, tile_rows, width), targets, axis=0)]
  transfers between devices with their start and end apart: 6 -> 0, of which waited for: 2 -> 0; matrix products, arithmetic and copies ran while one was open for 4% -> 0% of each run, Pallas kernels for 0% -> 0%
where the time goes in v1:
time: 42.5 us; the launch traced here: 42.2 us
  Pallas kernels  31.9 us (75%)
  local copies, waits for them, and re-layouts  8.28 us (19%)
  between operations  1.96 us (5%)
    pallas_call x1, Pallas kernels, per_device(): pl.pallas_call(functools.partial(kernel, doms, clusters), out_shape=(jax....  31.9 us
    unnamed x19, local copies, waits for them, and re-layouts  8.28 us

profile of v1, /device:TPU:0, one launch (start us, length us, event | category | flops | bytes accessed | tf_op | source)
XLA Modules:
  0.0 42.2 jit_solution(8329395224847766083)
XLA Ops:
  1.9 0.0 copy-start.5
  1.9 0.0 copy-start.6
  1.9 0.0 copy-start.7
  2.0 0.6 %copy-done.5 = s32[1,8]{1,0:T(1,128)S(1)} copy-done((s32[1,8]{1,0:T(1,128)S(1)}, s32[1,8]{1,0:T(1,128)}, u32[]{:S(2)}) %copy-start.5) | copy-done | bytes 56
  2.6 0.0 copy-done.6
  2.6 0.0 copy-done.7
  2.6 0.0 copy-start
  2.6 1.1 %copy-done = bf16[1,768,512]{2,1,0:T(8,128)(2,1)S(1)} copy-done((bf16[1,768,512]{2,1,0:T(8,128)(2,1)S(1)}, bf16[1,768,512]{2,1,0:T(8,128)(2,1)}, u32[]{:S(2)}) %copy-start) | copy-done | bytes 786456
  3.7 0.0 copy-start.1
  3.7 1.1 %copy-done.1 = bf16[1,768,512]{2,1,0:T(8,128)(2,1)S(1)} copy-done((bf16[1,768,512]{2,1,0:T(8,128)(2,1)S(1)}, bf16[1,768,512]{2,1,0:T(8,128)(2,1)}, u32[]{:S(2)}) %copy-start.1) | copy-done | bytes 786456
  4.9 0.0 copy-start.2
  4.9 1.0 %copy-done.2 = bf16[512,512]{1,0:T(8,128)(2,1)S(1)} copy-done((bf16[512,512]{1,0:T(8,128)(2,1)S(1)}, bf16[512,512]{1,0:T(8,128)(2,1)}, u32[]{:S(2)}) %copy-start.2) | copy-done | bytes 524312
  5.9 0.0 copy-start.3
  5.9 0.9 %copy-done.3 = bf16[1,32,32,128]{3,2,1,0:T(8,128)(2,1)S(1)} copy-done((bf16[1,32,32,128]{3,2,1,0:T(8,128)(2,1)S(1)}, bf16[1,32,32,128]{3,2,1,0:T(8,128)(2,1)}, u32[]{:S(2)}) %copy-start.3) | copy-done | bytes 262168
  6.9 0.0 copy-start.4
  6.9 0.9 %copy-done.4 = bf16[1,256,512]{2,1,0:T(8,128)(2,1)S(1)} copy-done((bf16[1,256,512]{2,1,0:T(8,128)(2,1)S(1)}, bf16[1,256,512]{2,1,0:T(8,128)(2,1)}, u32[]{:S(2)}) %copy-start.4) | copy-done | bytes 262168
  7.8 31.9 %shard_map.121 = (bf16[768,512]{1,0:T(8,128)(2,1)S(1)}, bf16[768,512]{1,0:T(8,128)(2,1)S(1)}, f32[64,512]{1,0:T(8,128)S(1)}) custom-call(s32[1,1]{1,0:T(1,128)S(6)} %copy.16.bnd, s32[1,8]{1,0:T(1,128)S(1)} %copy-done.5, s32[1,32]{1,0:T(1,128)S(1)} %copy-done.6, s32[1,32]{1,0:T(1,128)S(1)} %copy-done.7, s32[1,1]{1,0:T(1,128)S(6)} %copy.17.tcnt, ...), custom_call_target="tpu_custom_call" | custom-call | tf_op jit(solution)/shard_map/pallas_call | solution.py:260
  39.7 0.9 %copy.18 = bf16[1,768,512]{2,1,0:T(8,128)(2,1)} copy(bf16[1,768,512]{2,1,0:T(8,128)(2,1)S(1)} %bitcast.7) | data formatting | bytes 1572864
  40.6 0.9 %copy.19 = bf16[1,768,512]{2,1,0:T(8,128)(2,1)} copy(bf16[1,768,512]{2,1,0:T(8,128)(2,1)S(1)} %bitcast.6) | data formatting | bytes 1572864
  41.5 0.7 %copy.20 = f32[64,512]{1,0:T(8,128)} copy(f32[64,512]{1,0:T(8,128)S(1)} %get-tuple-element.14) | data formatting | bytes 262144
Async XLA Ops:
  1.9 0.7 %copy-start.5 = (s32[1,8]{1,0:T(1,128)S(1)}, s32[1,8]{1,0:T(1,128)}, u32[]{:S(2)}) copy-start(s32[1,8]{1,0:T(1,128)} %skip.1) | copy-start | bytes 100
  1.9 0.7 %copy-start.6 = (s32[1,32]{1,0:T(1,128)S(1)}, s32[1,32]{1,0:T(1,128)}, u32[]{:S(2)}) copy-start(s32[1,32]{1,0:T(1,128)} %trow.1) | copy-start | bytes 388
  1.9 0.7 %copy-start.7 = (s32[1,32]{1,0:T(1,128)S(1)}, s32[1,32]{1,0:T(1,128)}, u32[]{:S(2)}) copy-start(s32[1,32]{1,0:T(1,128)} %tsrc.1) | copy-start | bytes 388
  2.6 1.1 %copy-start = (bf16[1,768,512]{2,1,0:T(8,128)(2,1)S(1)}, bf16[1,768,512]{2,1,0:T(8,128)(2,1)}, u32[]{:S(2)}) copy-start(bf16[1,768,512]{2,1,0:T(8,128)(2,1)} %param.10) | copy-start | bytes 2359300
  3.7 1.1 %copy-start.1 = (bf16[1,768,512]{2,1,0:T(8,128)(2,1)S(1)}, bf16[1,768,512]{2,1,0:T(8,128)(2,1)}, u32[]{:S(2)}) copy-start(bf16[1,768,512]{2,1,0:T(8,128)(2,1)} %param.19) | copy-start | bytes 2359300
  4.9 1.0 %copy-start.2 = (bf16[512,512]{1,0:T(8,128)(2,1)S(1)}, bf16[512,512]{1,0:T(8,128)(2,1)}, u32[]{:S(2)}) copy-start(bf16[512,512]{1,0:T(8,128)(2,1)} %weight_h.1) | copy-start | bytes 1572868
  5.9 0.9 %copy-start.3 = (bf16[1,32,32,128]{3,2,1,0:T(8,128)(2,1)S(1)}, bf16[1,32,32,128]{3,2,1,0:T(8,128)(2,1)}, u32[]{:S(2)}) copy-start(bf16[1,32,32,128]{3,2,1,0:T(8,128)(2,1)} %param.14) | copy-start | bytes 786436
  6.9 0.9 %copy-start.4 = (bf16[1,256,512]{2,1,0:T(8,128)(2,1)S(1)}, bf16[1,256,512]{2,1,0:T(8,128)(2,1)}, u32[]{:S(2)}) copy-start(bf16[1,256,512]{2,1,0:T(8,128)(2,1)} %param.11) | copy-start | bytes 786436

commit v2 on v1

--- a/solution.py
+++ b/solution.py
@@ -110,15 +110,25 @@
         copy.start()
         return copy
 
-    gathers = []
-    for k in range(1, doms):
-        gathers.append(
-            remote(own, gath.at[k], ag_send.at[k], ag_recv.at[k], dom_at(k))
-        )
+    gathers = {}
+
+    def gather(src, slot, to):
+        return remote(src, gath.at[slot], ag_send.at[slot], ag_recv.at[slot], to)
+
+    aside = 1 - 2 * lax.rem(me, 2)
+    pair_to = {"dom": me + aside}
+
+    def forward(k):
+        slot = lax.rem(k + aside + doms, doms)
+        src = own if k == 0 else gath.at[k]
+        return gather(src, slot, pair_to)
+
+    near = list(range(2, doms, 2))
+    for k in near:
+        gathers[k] = gather(own, k, dom_at(k))
+    forwards = [forward(0)]
     for k, by in ((doms, 1), (doms + 1, -1)):
-        gathers.append(
-            remote(own, gath.at[k], ag_send.at[k], ag_recv.at[k], cluster_at(by))
-        )
+        gathers[k] = gather(own, k, cluster_at(by))
 
     loads[1].wait()
     sources = (doms + 2) * blk
@@ -130,6 +140,9 @@
         row = trow[0, t] + nodes * jnp.maximum(t + 1 - tcnt[0, 0], 0)
         block = jnp.concatenate([tiles[t].astype(F32)] * row_blocks, axis=1)
         spread[at, :] = jnp.where(row_block == row, block, 0.0).astype(BF16)
+    for k in sorted(near, key=lambda k: min(k, doms - k)):
+        gathers[k].wait_recv()
+        forwards.append(forward(k))
     adj[...] = dot(picks[...], spread[...], 0, 0).astype(BF16)
 
     loads[2].wait()
@@ -142,8 +155,10 @@
         return source, pl.ds(pl.multiple_of(source * blk, blk), blk)
 
     for k in range(doms + 2):
-        if k > 0:
-            gathers[k - 1].wait_recv()
+        if k >= doms:
+            gathers[k].wait_recv()
+        elif k % 2 == 1:
+            pltpu.make_async_copy(gath.at[k], gath.at[k], ag_recv.at[k]).wait()
         fresh = own[...] if k == 0 else gath[k]
         source, at = block_of(k)
         if k < doms:
@@ -169,6 +184,21 @@
     half_out[...] = dot(agg[...], dz[:, half_at(1 - parity)], 0, 0).astype(BF16)
     partner = {"cluster": mine + 1 - 2 * parity}
     halves = remote(half_out, half_in, half_send.at[0], half_recv.at[0], partner)
+
+    wsum = dot(agg[...], dz[:, half_at(parity)], 0, 0)
+    halves.wait_recv()
+    wsum = wsum + half_in[...].astype(F32)
+    pair[...] = wsum.astype(BF16)
+
+    def share_at(k):
+        part = lax.rem(me + k + doms, doms)
+        return pl.ds(pl.multiple_of(part * share, share), share)
+
+    pairs = []
+    for k in range(1, doms):
+        pairs.append(
+            remote(pair.at[share_at(k)], pair_in.at[k], pair_send.at[k], pair_recv.at[k], dom_at(k))
+        )
 
     for r in range(0, nodes, chunk):
         rows = slice(r, r + chunk)
@@ -187,30 +217,6 @@
             remote(bg_out.at[block_of(k)[1]], bg_in.at[k], bg_send.at[k], bg_recv.at[k], to)
         )
 
-    wsum = dot(agg[...], dz[:, half_at(parity)], 0, 0)
-    halves.wait_recv()
-    wsum = wsum + half_in[...].astype(F32)
-    pair[...] = wsum.astype(BF16)
-
-    def share_at(k):
-        part = lax.rem(me + k + doms, doms)
-        return pl.ds(pl.multiple_of(part * share, share), share)
-
-    pairs = []
-    for k in range(1, doms):
-        pairs.append(
-            remote(pair.at[share_at(k)], pair_in.at[k], pair_send.at[k], pair_recv.at[k], dom_at(k))
-        )
-
-    bgrad = bg_out[block_of(0)[1], :].astype(F32)
-    for k in range(1, doms + 2):
-        blocks[k - 1].wait_recv()
-        bgrad = bgrad + bg_in[k].astype(F32)
-    for b in range(nodes // blk):
-        rows = slice(b * blk, (b + 1) * blk)
-        here = jnp.where(one * b == bnd[0, 0], bgrad, 0.0)
-        gfeat[rows, :] = (dagg[rows, :].astype(F32) + here).astype(BF16)
-
     rsum = pair[share_at(0), :].astype(F32)
     for k in range(1, doms):
         pairs[k - 1].wait_recv()
@@ -221,6 +227,15 @@
         quarters.append(
             remote(quarter, quarter_in.at[k], q_send.at[k], q_recv.at[k], cluster_at(k))
         )
+    bgrad = bg_out[block_of(0)[1], :].astype(F32)
+    for k in range(1, doms + 2):
+        blocks[k - 1].wait_recv()
+        bgrad = bgrad + bg_in[k].astype(F32)
+    for b in range(nodes // blk):
+        rows = slice(b * blk, (b + 1) * blk)
+        here = jnp.where(one * b == bnd[0, 0], bgrad, 0.0)
+        gfeat[rows, :] = (dagg[rows, :].astype(F32) + here).astype(BF16)
+
     same = quarter[...].astype(F32)
     other = jnp.zeros_like(same)
     for k in range(1, clusters):
@@ -232,7 +247,7 @@
     gw[:, half_at(parity)] = same
     gw[:, half_at(1 - parity)] = other
 
-    for copy in gathers + [halves] + blocks + pairs + quarters:
+    for copy in list(gathers.values()) + forwards + [halves] + blocks + pairs + quarters:
         copy.wait_send()
 
 
@@ -255,7 +270,7 @@
     half, share = width // 2, width // doms
     smem = pl.BlockSpec(memory_space=pltpu.SMEM)
     vmem = pl.BlockSpec(memory_space=pltpu.VMEM)
-    hbm = pl.BlockSpec(memory_space=pl.ANY)
+    hbm = pl.BlockSpec(memory_space=pltpu.HBM)
     dma = pltpu.SemaphoreType.DMA
     out, gfeat, gw = pl.pallas_call(
         functools.partial(kernel, doms, clusters),
@@ -302,7 +317,7 @@
             dma((clusters,)),
         ],
         compiler_params=pltpu.CompilerParams(
-            collective_id=0, has_side_effects=True, vmem_limit_bytes=40 * 2**20
+            collective_id=0, has_side_effects=True, vmem_limit_bytes=62 * 2**20
         ),
     )(
         boundary,

time: 42.5 us -> 38.1 us (0.90)
  local copies, waits for them, and re-layouts: 8.28 us -> 3.82 us
    unnamed x19 -> x7, local copies, waits for them, and re-layouts: 8.28 us -> 3.82 us
where the time goes in v2:
time: 38.1 us; the launch traced here: 37.8 us
  Pallas kernels  32 us (84%)
  local copies, waits for them, and re-layouts  3.82 us (10%)
  between operations  1.94 us (5%)
    pallas_call x1, Pallas kernels, per_device(): pl.pallas_call(functools.partial(kernel, doms, clusters), out_shape=(jax....  32 us
    unnamed x7, local copies, waits for them, and re-layouts  3.82 us

profile of v2, /device:TPU:0, one launch (start us, length us, event | category | flops | bytes accessed | tf_op | source)
XLA Modules:
  0.0 37.8 jit_solution(6043995760187631652)
XLA Ops:
  1.9 32.0 %shard_map.121 = (bf16[768,512]{1,0:T(8,128)(2,1)}, bf16[768,512]{1,0:T(8,128)(2,1)}, f32[64,512]{1,0:T(8,128)}) custom-call(s32[1,1]{1,0:T(1,128)S(6)} %copy.16.bnd, s32[1,8]{1,0:T(1,128)} %skip.1, s32[1,32]{1,0:T(1,128)} %trow.1, s32[1,32]{1,0:T(1,128)} %tsrc.1, s32[1,1]{1,0:T(1,128)S(6)} %copy.17.tcnt, bf16[768,512]{1,0:T(8,128)(2,1)} %bitcast.8, ...), custom_call_target="tpu_custom_call" | custom-call | tf_op jit(solution)/shard_map/pallas_call | solution.py:275
  34.0 0.0 copy-start
  34.0 2.1 %copy.18 = bf16[1,768,512]{2,1,0:T(8,128)(2,1)} copy(bf16[1,768,512]{2,1,0:T(8,128)(2,1)} %bitcast.7) | data formatting | bytes 1572864
  36.1 0.0 copy-done
  36.1 0.0 copy-start.1
  36.1 0.9 %copy.19 = bf16[1,768,512]{2,1,0:T(8,128)(2,1)} copy(bf16[1,768,512]{2,1,0:T(8,128)(2,1)S(1)} %bitcast.6) | data formatting | bytes 1572864
  37.0 0.1 copy-done.1
  37.1 0.7 %copy.20 = f32[64,512]{1,0:T(8,128)} copy(f32[64,512]{1,0:T(8,128)S(1)} %copy-done.1) | data formatting | bytes 262144
Async XLA Ops:
  34.0 2.1 %copy-start = (bf16[768,512]{1,0:T(8,128)(2,1)S(1)}, bf16[768,512]{1,0:T(8,128)(2,1)}, u32[]{:S(2)}) copy-start(bf16[768,512]{1,0:T(8,128)(2,1)} %get-tuple-element.7) | copy-start | bytes 2359300
  36.1 1.0 %copy-start.1 = (f32[64,512]{1,0:T(8,128)S(1)}, f32[64,512]{1,0:T(8,128)}, u32[]{:S(2)}) copy-start(f32[64,512]{1,0:T(8,128)} %get-tuple-element.14) | copy-start | bytes 393220
